TPU v7x, 32 devices: a whole 2x2x4 slice. The times are simulated.
32 devices in a mesh: row: 8 (over y, x, core), col: 4 (over z).
Axes of the slice: x: 2, y: 2, z: 4, core: 2. Of those that a mesh axis runs over, the one named last changes fastest.
Arguments:
- tokens: bfloat16 [128, 96, 768], P('row', 'col'), as said below
- dw_kernel: float32 [7, 7, 768], replicated, may hold values from -0.875 to 0.875
- norm_gain: float32 [768], replicated, may hold values from 0.5 to 1.5
- norm_shift: float32 [768], replicated, may hold values from -3 to 3
- w_in: bfloat16 [768, 3072], P(None, 'col'), may hold values from -0.21875 to 0.21875
- w_out: bfloat16 [3072, 768], P('col'), may hold values from -0.109375 to 0.109375
- w_kv: bfloat16 [768, 1536], P(None, 'col'), as said below
- queries: bfloat16 [512, 768], replicated, may hold values from -300 to 300, as said below
- latent_gain: float32 [768], replicated, may hold values from 0.5 to 1.5
- w_o: bfloat16 [768, 768], P(None, 'col'), may hold values from -0.21875 to 0.21875
Outputs:
- token_map: bfloat16 [128, 96, 768], P('row', 'col')
- latents: bfloat16 [512, 768], replicated
Inputs may be any that keep to these rules, and one draw needn't show every extreme that they name: Latent queries; a few rows may be far larger than the others. `tokens`: patch token features, roughly unit normal, between -24 and 24; a few cells hold 24 in two channels. `w_kv`: key and value projection weights.
All inputs are finite; a program needn't handle non-finite values.
Results may differ from a plain program's by a relative error of at most 0.011.
Values may be sent and summed in bfloat16 or wider, within the bound.
A program may use at most 64 MiB of HBM per device.

v0:
```python
import math
import jax
import jax.numpy as jnp
from jax import lax
from jax.sharding import PartitionSpec as P

HEADS = 12
HEAD = 64


def with_halo(cells, sides, width):
    for axis, dim in sides:
        count = lax.axis_size(axis)
        ends = count - 1
        head = lax.slice_in_dim(cells, 0, width, axis=dim)
        tail = lax.slice_in_dim(cells, cells.shape[dim] - width, cells.shape[dim], axis=dim)
        cells = jnp.concatenate(
            [
                lax.ppermute(tail, axis, [(i, (i + 1) % count) for i in range(ends)]),
                cells,
                lax.ppermute(head, axis, [((i + 1) % count, i) for i in range(ends)]),
            ],
            axis=dim,
        )
    return cells


def conv_taps(padded, height, width, dw_kernel):
    mixed = jnp.zeros((height, width, padded.shape[2]), jnp.float32)
    for row_tap in range(7):
        for col_tap in range(7):
            mixed = (
                mixed
                + padded[row_tap : row_tap + height, col_tap : col_tap + width]
                * dw_kernel[row_tap, col_tap]
            )
    return mixed


def layer_norm(mixed, norm_gain, norm_shift):
    center = mixed - jnp.mean(mixed, axis=-1, keepdims=True)
    spread = jnp.mean(center * center, axis=-1, keepdims=True)
    return (center * lax.rsqrt(spread + 1e-06) * norm_gain + norm_shift).astype(jnp.bfloat16)


def finish_latents(numer, denom, latent_gain, w_full):
    attended = (numer / denom[..., None]).reshape(numer.shape[0], -1)
    squares = jnp.mean(attended * attended, axis=-1, keepdims=True)
    scaled = (attended * lax.rsqrt(squares + 1e-06) * latent_gain).astype(jnp.bfloat16)
    return jnp.dot(scaled, w_full, preferred_element_type=jnp.float32).astype(jnp.bfloat16)


def body(tokens, dw_kernel, norm_gain, norm_shift, w_in, w_out, w_kv, queries, latent_gain, w_o):
    height, width, width_d = tokens.shape
    latent_count = queries.shape[0]
    padded = with_halo(tokens, (("row", 0), ("col", 1)), 3)
    mixed = conv_taps(padded.astype(jnp.float32), height, width, dw_kernel)
    normed = layer_norm(mixed, norm_gain, norm_shift).reshape(height * width, width_d)
    residual = tokens.reshape(height * width, width_d).astype(jnp.float32)
    hidden = jax.nn.gelu(
        jnp.dot(
            normed,
            lax.all_gather(w_in, "col", axis=1, tiled=True),
            preferred_element_type=jnp.float32,
        )
    ).astype(jnp.bfloat16)
    update = jnp.dot(
        hidden, lax.all_gather(w_out, "col", axis=0, tiled=True), preferred_element_type=jnp.float32
    )
    token_rows = (residual + update).astype(jnp.bfloat16)
    token_map = token_rows.reshape(height, width, width_d)
    keys_vals = jnp.dot(
        token_rows,
        lax.all_gather(w_kv, "col", axis=1, tiled=True),
        preferred_element_type=jnp.float32,
    ).astype(jnp.bfloat16)
    w_full = lax.all_gather(w_o, "col", axis=1, tiled=True)
    key_heads = keys_vals[:, :width_d].reshape(-1, HEADS, HEAD)
    val_heads = keys_vals[:, width_d:].reshape(-1, HEADS, HEAD)
    query_heads = queries.reshape(latent_count, HEADS, HEAD)
    score_scale = 1.0 / math.sqrt(HEAD)
    group_size = math.gcd(HEADS, 4)
    max_parts, den_parts, num_parts = ([], [], [])
    for first_head in range(0, HEADS, group_size):
        scores = (
            jnp.einsum(
                "lhd,thd->lht",
                query_heads[:, first_head : first_head + group_size],
                key_heads[:, first_head : first_head + group_size],
                preferred_element_type=jnp.float32,
            )
            * score_scale
        )
        local_max = jnp.max(scores, axis=-1)
        weights = jnp.exp(scores - local_max[..., None])
        den_parts.append(jnp.sum(weights, axis=-1))
        max_parts.append(local_max)
        num_parts.append(
            jnp.einsum(
                "lht,thd->lhd",
                weights.astype(jnp.bfloat16),
                val_heads[:, first_head : first_head + group_size],
                preferred_element_type=jnp.float32,
            )
        )
    maxima = jnp.concatenate(max_parts, axis=1)
    denom = jnp.concatenate(den_parts, axis=1)
    numer = jnp.concatenate(num_parts, axis=1)
    peak = lax.pmax(maxima, ("row", "col"))
    factor = jnp.exp(maxima - peak)
    den_terms = denom * factor
    num_terms = (numer * factor[..., None]).reshape(latent_count, width_d)
    den_part, num_part = (
        lax.psum_scatter(den_terms, "col", scatter_dimension=0, tiled=True),
        lax.psum_scatter(num_terms, "col", scatter_dimension=0, tiled=True),
    )
    den_share, num_share = lax.psum((den_part, num_part), "row")
    own_rows = finish_latents(
        num_share.reshape(num_share.shape[0], HEADS, HEAD), den_share, latent_gain, w_full
    )
    latents = lax.all_gather(own_rows, "col", axis=0, tiled=True)
    return (token_map, latents)


def solution(mesh):
    in_specs = (
        P("row", "col", None),
        P(),
        P(),
        P(),
        P(None, "col"),
        P("col", None),
        P(None, "col"),
        P(),
        P(),
        P(None, "col"),
    )
    out_specs = (P("row", "col", None), P())
    return jax.shard_map(body, mesh=mesh, in_specs=in_specs, out_specs=out_specs, check_vma=False)
```

profile of v0, /device:TPU:0, one launch (start us, length us, event | category | flops | bytes accessed | tf_op | source)
XLA Modules:
  0.0 479.7 jit_solution(5248755326156885472)
XLA Ops:
  7.2 0.7 all-gather.5.cloned.1.call-update
  8.0 0.7 all-gather.7.cloned.1.call-update
  8.8 2.4 collective-permute-start
  11.2 1.3 collective-permute-start.1
  12.6 0.2 slice_reduce_fusion.47
  12.7 1.2 copy.24
  13.9 0.2 slice_reduce_fusion.48
  14.1 2.3 collective-permute-done.1
  16.5 0.1 fusion.112
  16.6 3.5 collective-permute-start.2
  20.1 1.3 collective-permute-start.3
  21.5 4.3 collective-permute-done.2
  25.8 7.4 %collective-permute-done.3 = bf16[22,3,768]{2,1,0:T(4,128)(2,1)S(1)} collective-permute-done((bf16[22,3,768]{2,1,0:T(4,128)(2,1)S(1)}, bf16[22,3,768]{2,1,0:T(4,128)(2,1)S(1)}, u32[]{:S(2)}, u32[]{:S(2)}) %collective-permute-start.3) | collective-permute-done | bytes 101408 | tf_op jit(solution)/shard_map/ppermute | solution.py:21
  33.2 0.4 maximum_convert_fusion
  33.6 12.3 %fusion.109 = (f32[16,24]{1,0:T(8,128)S(1)}, f32[16,24,768]{2,1,0:T(8,128)S(1)}) fusion(f32[768]{0:T(1024)S(1)} %get-tuple-element.49, f32[22,30,768]{2,1,0:T(8,128)S(1)} %maximum_convert_fusion, f32[768]{0:T(1024)S(1)} %get-tuple-element.50, f32[768]{0:T(1024)S(1)} %get-tuple-element.3, f32[768]{0:T(1024)S(1)} %get-tuple-element.4, ...), kind=kLoop, calls=%fused_computation.218 | loop fusion | flops 28900992 | bytes 59134464 | tf_op jit(solution)/shard_map/reduce_sum | solution.py:41
  45.9 0.3 multiply_reduce_fusion
  46.2 0.4 copy-done.7
  46.6 0.3 add_convert_fusion
  46.8 57.7 %all-gather.5.cloned.1.call-done = bf16[768,3072]{1,0:T(8,128)(2,1)} async-done(((bf16[768,768]{1,0:T(8,128)(2,1)}), bf16[768,3072]{1,0:T(8,128)(2,1)}) %all-gather.5.cloned.1.call-update) | async-done | bytes 4718608 | tf_op jit(solution)/shard_map/all_gather | solution.py:63
  104.6 89.4 %all-gather.7.cloned.1.call-done = bf16[3072,768]{1,0:T(8,128)(2,1)} async-done(((bf16[768,768]{1,0:T(8,128)(2,1)}), bf16[3072,768]{1,0:T(8,128)(2,1)}) %all-gather.7.cloned.1.call-update) | async-done | bytes 4718608 | tf_op jit(solution)/shard_map/all_gather | solution.py:68
  193.9 7.9 %fusion.34 = bf16[384,768]{1,0:T(8,128)(2,1)S(1)} fusion(bf16[3072,768]{1,0:T(8,128)(2,1)} %all-gather.7.cloned.1.call-done, bf16[384,768]{1,0:T(8,128)(2,1)S(1)} %bitcast.66, bf16[384,768]{1,0:T(8,128)(2,1)S(1)} %bitcast.70, bf16[768,3072]{1,0:T(8,128)(2,1)} %all-gather.5.cloned.1.call-done), kind=kOutput, calls=%fused_computation.37 | convolution fusion | flops 3635380224 | bytes 11206656 | tf_op jit(solution)/shard_map/dot_general | solution.py:67
  201.9 42.4 %all-gather.9.cloned.1.call-done = bf16[768,1536]{1,0:T(8,128)(2,1)} async-done(((bf16[768,384]{1,0:T(8,128)(2,1)}), bf16[768,1536]{1,0:T(8,128)(2,1)}) %all-gather.9.cloned.1.call-update) | async-done | bytes 2359312 | tf_op jit(solution)/shard_map/all_gather | solution.py:74
  244.2 2.7 convolution_convert_fusion
  247.0 0.9 fusion.111
  247.9 1.0 copy.23
  248.9 1.8 bitcast_reduce_fusion
  250.8 2.3 bitcast_reduce_fusion.1
  253.0 2.3 bitcast_reduce_fusion.2
  255.4 2.1 copy.22
  257.5 3.6 fusion.37
  261.1 3.0 fusion.11
  264.1 1.5 fusion.40
  265.6 0.5 fusion.15
  266.2 1.5 fusion.43
  267.6 39.0 %pmax.7 = f32[512,12]{0,1:T(8,128)S(1)} all-reduce(f32[512,12]{0,1:T(8,128)S(1)} %pad_maximum_fusion), channel_id=1, replica_groups=mesh['row'=8,'col'=4] {'row','col'}, use_global_device_ids=true, to_apply=%region_5.0 | all-reduce | flops 6144 | bytes 49152 | tf_op jit(solution)/shard_map/pmax | solution.py:109
  306.7 0.6 maximum_multiply_fusion.1
  307.3 2.7 maximum_multiply_fusion
  310.0 0.5 reduce-scatter.5.cloned.1.call-update
  310.6 34.6 %reduce-scatter.3.cloned.1.call-done = f32[128,768]{0,1:T(8,128)} async-done(((f32[512,768]{0,1:T(8,128)}), f32[128,768]{0,1:T(8,128)}) %reduce-scatter.3.cloned.1.call-update) | async-done | bytes 393232 | tf_op jit(solution)/shard_map/reduce_scatter | solution.py:115
  345.3 0.7 all-gather.11.cloned.1.call-update
  346.0 19.4 %reduce-scatter.5.cloned.1.call-done = f32[128,12]{0,1:T(8,128)} async-done(((f32[512,12]{0,1:T(8,128)}), f32[128,12]{0,1:T(8,128)}) %reduce-scatter.5.cloned.1.call-update) | async-done | bytes 6160 | tf_op jit(solution)/shard_map/reduce_scatter | solution.py:114
  365.4 12.2 %psum.15 = f32[128,12]{0,1:T(8,128)S(1)} all-reduce(f32[128,12]{0,1:T(8,128)} %reduce-scatter.5.cloned.1.call-done), channel_id=1, replica_groups=mesh['row'=8,'col'=4] {'row'}, use_global_device_ids=true, to_apply=%region_12.0 | all-reduce | flops 1536 | bytes 12288 | tf_op jit(solution)/shard_map/psum | solution.py:117
  377.7 43.2 %all-reduce.2.cloned.1.call-done = f32[128,768]{0,1:T(8,128)} async-done(((f32[128,768]{0,1:T(8,128)}), f32[128,768]{0,1:T(8,128)}) %all-reduce.2.cloned.1.call-update) | async-done | bytes 393232 | tf_op jit(solution)/shard_map/psum | solution.py:117
  420.9 1.1 multiply_reduce_fusion.1
  422.0 30.1 %all-gather.11.cloned.1.call-done = bf16[768,768]{0,1:T(8,128)(2,1)} async-done(((bf16[768,192]{0,1:T(8,128)(2,1)}), bf16[768,768]{0,1:T(8,128)(2,1)}) %all-gather.11.cloned.1.call-update) | async-done | bytes 1179664 | tf_op jit(solution)/shard_map/all_gather | solution.py:77
  452.1 1.9 convolution_convert_fusion.1
  454.0 17.9 %all_gather.19 = bf16[512,768]{1,0:T(8,128)(2,1)S(1)} all-gather(bf16[128,768]{1,0:T(8,128)(2,1)S(1)} %convolution_convert_fusion.1), channel_id=1, replica_groups=mesh['row'=8,'col'=4] {'col'}, dimensions={0}, use_global_device_ids=true | all-gather | bytes 983040 | tf_op jit(solution)/shard_map/all_gather | solution.py:121
  471.9 0.9 copy.35
  (41 shorter events, 0.6 us)
Async XLA Ops:
  7.2 1.6 copy-start.1
  7.2 97.4 %all-gather.5.cloned.1.call-start = ((), (), s32[]{:S(2)}) async-start(), calls=%async_computation.2 | async-start | bytes 5898240 | tf_op jit(solution)/shard_map/all_gather | solution.py:63
  7.9 4.6 copy-start.6
  7.9 4.8 %copy-start.2 = (bf16[512,768]{1,0:T(8,128)(2,1)S(1)}, bf16[512,768]{1,0:T(8,128)(2,1)}, u32[]{:S(2)}) copy-start(bf16[512,768]{1,0:T(8,128)(2,1)} %param.17) | copy-start | bytes 2359300
  7.9 186.0 %all-gather.7.cloned.1.call-start = ((), (), s32[]{:S(2)}) async-start(), calls=%async_computation.3 | async-start | bytes 5898240 | tf_op jit(solution)/shard_map/all_gather | solution.py:68
  8.7 235.6 %all-gather.9.cloned.1.call-start = ((), (), s32[]{:S(2)}) async-start(), calls=%async_computation.4 | async-start | bytes 2949120 | tf_op jit(solution)/shard_map/all_gather | solution.py:74
  8.8 5.3 %collective-permute-start = (bf16[3,24,768]{2,1,0:T(8,128)(2,1)S(1)}, bf16[3,24,768]{2,1,0:T(8,128)(2,1)S(1)}, u32[]{:S(2)}, u32[]{:S(2)}) collective-permute-start(bf16[3,24,768]{2,1,0:T(8,128)(2,1)S(1)} %get-tuple-element.62), channel_id=1, source_target_pairs={{0,4},{4,8},{8,12},{12,16},{16,20},{20,24},{24,28},{1,5},{5,9},{9,... | collective-permute-start | bytes 331784 | tf_op jit(solution)/shard_map/ppermute | solution.py:19
  11.2 5.3 %collective-permute-start.1 = (bf16[3,24,768]{2,1,0:T(8,128)(2,1)S(1)}, bf16[3,24,768]{2,1,0:T(8,128)(2,1)S(1)}, u32[]{:S(2)}, u32[]{:S(2)}) collective-permute-start(bf16[3,24,768]{2,1,0:T(8,128)(2,1)S(1)} %get-tuple-element.61), channel_id=1, source_target_pairs={{4,0},{8,4},{12,8},{16,12},{20,16},{24,20},{28,24},{5,1},{9,5},{13... | collective-permute-start | bytes 331784 | tf_op jit(solution)/shard_map/ppermute | solution.py:21
  12.5 332.7 %reduce-scatter.3.cloned.1.call-start = ((), (), s32[]{:S(2)}) async-start(), calls=%async_computation.5 | async-start | bytes 1966080 | tf_op jit(solution)/shard_map/reduce_scatter | solution.py:115
  16.6 9.2 %collective-permute-start.2 = (bf16[22,3,768]{2,1,0:T(4,128)(2,1)S(1)}, bf16[22,3,768]{2,1,0:T(4,128)(2,1)S(1)}, u32[]{:S(2)}, u32[]{:S(2)}) collective-permute-start(bf16[22,3,768]{2,1,0:T(4,128)(2,1)S(1)} %get-tuple-element.59), channel_id=1, source_target_pairs={{0,1},{1,2},{2,3},{4,5},{5,6},{6,7},{8,9},{9,10},{10,11},{12,13},{... | collective-permute-start | bytes 304136 | tf_op jit(solution)/shard_map/ppermute | solution.py:19
  20.1 13.1 %collective-permute-start.3 = (bf16[22,3,768]{2,1,0:T(4,128)(2,1)S(1)}, bf16[22,3,768]{2,1,0:T(4,128)(2,1)S(1)}, u32[]{:S(2)}, u32[]{:S(2)}) collective-permute-start(bf16[22,3,768]{2,1,0:T(4,128)(2,1)S(1)} %get-tuple-element.60), channel_id=1, source_target_pairs={{1,0},{2,1},{3,2},{5,4},{6,5},{7,6},{9,8},{10,9},{11,10},{13,12},{... | collective-permute-start | bytes 304136 | tf_op jit(solution)/shard_map/ppermute | solution.py:21
  45.9 0.7 copy-start.7
  45.9 0.7 copy-start.8
  201.9 45.1 %copy-start.10 = (bf16[384,768]{1,0:T(8,128)(2,1)}, bf16[384,768]{1,0:T(8,128)(2,1)S(1)}, u32[]{:S(2)}) copy-start(bf16[384,768]{1,0:T(8,128)(2,1)S(1)} %fusion.34) | copy-start | bytes 1769476
  248.9 1.8 copy-start.3
  248.9 1.8 copy-start.5
  257.5 3.6 copy-start
  261.1 3.0 copy-start.4
  310.0 142.2 %copy-start.9 = (f32[768]{0:T(1024)S(1)}, f32[768]{0:T(1024)}, u32[]{:S(2)}) copy-start(f32[768]{0:T(1024)} %param.18) | copy-start | bytes 9220
  310.0 55.4 %reduce-scatter.5.cloned.1.call-start = ((), (), s32[]{:S(2)}) async-start(), calls=%async_computation.7 | async-start | bytes 40960 | tf_op jit(solution)/shard_map/reduce_scatter | solution.py:114
  310.6 110.3 %all-reduce.2.cloned.1.call-start = ((), (), s32[]{:S(2)}) async-start(), calls=%async_computation.6 | async-start | bytes 786432 | tf_op jit(solution)/shard_map/psum | solution.py:117
  345.2 106.9 %all-gather.11.cloned.1.call-start = ((), (), s32[]{:S(2)}) async-start(), calls=%async_computation.8 | async-start | bytes 1474560 | tf_op jit(solution)/shard_map/all_gather | solution.py:77
Sparse Core Ops, SparseCore 0:
  9.6 94.9 all-gather.4
  106.1 87.7 all-gather.6
  195.6 48.6 all-gather.8
  310.1 35.0 reduce-scatter.2
  347.3 18.0 reduce-scatter.4
  368.4 52.5 all-reduce.1
  422.5 29.6 all-gather.10
where the time goes:
time: 480 us
  waiting for transfers between devices  334 us (70%)
  blocking collectives  69.1 us (14%)
  matrix products  25.5 us (5%)
  other arithmetic  21.2 us (4%)
  between operations  14.4 us (3%)
  starting transfers between devices  8.75 us (2%)
  local copies, waits for them, and re-layouts  7.14 us (1%)
    all_gather x1, waiting for transfers between devices, body(): lax.all_gather(w_out, 'col', axis=0, tiled=True)  89.4 us
    all_gather x1, waiting for transfers between devices, body(): lax.all_gather(w_in, 'col', axis=1, tiled=True)  57.7 us
    psum x1, waiting for transfers between devices, body(): den_share, num_share = lax.psum((den_part, num_part), 'row')  43.2 us
    all_gather x1, waiting for transfers between devices, body(): lax.all_gather(w_kv, 'col', axis=1, tiled=True)  42.4 us
    pmax x1, blocking collectives, body(): peak = lax.pmax(maxima, ('row', 'col'))  39 us
    reduce_scatter x1, waiting for transfers between devices, body(): lax.psum_scatter(num_terms, 'col', scatter_dimension=0, tiled=True)  34.6 us
    all_gather x1, waiting for transfers between devices, body(): w_full = lax.all_gather(w_o, 'col', axis=1, tiled=True)  30.1 us
    reduce_scatter x1, waiting for transfers between devices, body(): lax.psum_scatter(den_terms, 'col', scatter_dimension=0, tiled=True)  19.4 us
  transfers between devices with their start and end apart: 11, of which 10 were waited for; matrix products, arithmetic and copies ran while one was open for 5% of the time, Pallas kernels for 0%

commit v1 on v0

--- a/solution.py
+++ b/solution.py
@@ -6,6 +6,12 @@
 
 HEADS = 12
 HEAD = 64
+
+
+def in_order(parts, dim):
+    lengths = list(parts.shape[1:])
+    lengths[dim] *= parts.shape[0]
+    return jnp.moveaxis(parts, 0, dim).reshape(lengths)
 
 
 def with_halo(cells, sides, width):
@@ -74,7 +80,14 @@
         lax.all_gather(w_kv, "col", axis=1, tiled=True),
         preferred_element_type=jnp.float32,
     ).astype(jnp.bfloat16)
-    w_full = lax.all_gather(w_o, "col", axis=1, tiled=True)
+    size = lax.axis_size("col")
+    forward = [(i_2, (i_2 + 1) % size) for i_2 in range(size)]
+    blocks = [w_o]
+    while len(blocks) < size:
+        blocks.append(lax.ppermute(blocks[-1], "col", forward))
+    position = lax.axis_index("col")
+    blocks = jnp.stack(blocks)[(position - jnp.arange(size)) % size]
+    w_full = in_order(blocks, 1)
     key_heads = keys_vals[:, :width_d].reshape(-1, HEADS, HEAD)
     val_heads = keys_vals[:, width_d:].reshape(-1, HEADS, HEAD)
     query_heads = queries.reshape(latent_count, HEADS, HEAD)

time: 480 us -> 465 us (0.969)
  waiting for transfers between devices: 334 us -> 308 us
  starting transfers between devices: 8.75 us -> 16.8 us
    all_gather x1 -> x0, waiting for transfers between devices: 30.1 us -> none  [body(): w_full = lax.all_gather(w_o, 'col', axis=1, tiled=True)]
    ppermute x0 -> x3, waiting for transfers between devices: none -> 24.6 us  [body(): blocks.append(lax.ppermute(blocks[-1], 'col', forward))]
    reduce_scatter x1, waiting for transfers between devices: 34.6 us -> 16 us  [body(): lax.psum_scatter(num_terms, 'col', scatter_dimension=0, tiled=True)]
    ppermute x0 -> x3, starting transfers between devices: none -> 8.11 us  [body(): blocks.append(lax.ppermute(blocks[-1], 'col', forward))]
  transfers between devices with their start and end apart: 11 -> 13, of which waited for: 10 -> 11; matrix products, arithmetic and copies ran while one was open for 5% -> 5% of each run, Pallas kernels for 0% -> 0%
where the time goes in v1:
time: 465 us
  waiting for transfers between devices  308 us (66%)
  blocking collectives  70.7 us (15%)
  matrix products  24.2 us (5%)
  other arithmetic  21.3 us (5%)
  starting transfers between devices  16.8 us (4%)
  between operations  14.5 us (3%)
  local copies, waits for them, and re-layouts  8.66 us (2%)
    all_gather x1, waiting for transfers between devices, body(): lax.all_gather(w_out, 'col', axis=0, tiled=True)  89.4 us
    all_gather x1, waiting for transfers between devices, body(): lax.all_gather(w_in, 'col', axis=1, tiled=True)  57.7 us
    psum x1, waiting for transfers between devices, body(): den_share, num_share = lax.psum((den_part, num_part), 'row')  43.3 us
    all_gather x1, waiting for transfers between devices, body(): lax.all_gather(w_kv, 'col', axis=1, tiled=True)  42.4 us
    pmax x1, blocking collectives, body(): peak = lax.pmax(maxima, ('row', 'col'))  39 us
    ppermute x3, waiting for transfers between devices, body(): blocks.append(lax.ppermute(blocks[-1], 'col', forward))  24.6 us
    reduce_scatter x1, waiting for transfers between devices, body(): lax.psum_scatter(den_terms, 'col', scatter_dimension=0, tiled=True)  19.6 us
    all_gather x1, blocking collectives, body(): latents = lax.all_gather(own_rows, 'col', axis=0, tiled=True)  19.5 us
  transfers between devices with their start and end apart: 13, of which 11 were waited for; matrix products, arithmetic and copies ran while one was open for 5% of the time, Pallas kernels for 0%

profile of v1, /device:TPU:0, one launch (start us, length us, event | category | flops | bytes accessed | tf_op | source)
XLA Modules:
  0.0 464.7 jit_solution(7584691104339381945)
XLA Ops:
  7.2 0.7 all-gather.4.cloned.1.call-update
  8.0 0.7 all-gather.6.cloned.1.call-update
  8.8 2.4 collective-permute-start
  11.2 1.3 collective-permute-start.1
  12.7 1.2 copy.24
  14.1 2.3 collective-permute-done.1
  16.6 3.5 collective-permute-start.2
  20.1 1.3 collective-permute-start.3
  21.5 4.3 collective-permute-done.2
  25.8 7.4 %collective-permute-done.3 = bf16[22,3,768]{2,1,0:T(4,128)(2,1)S(1)} collective-permute-done((bf16[22,3,768]{2,1,0:T(4,128)(2,1)S(1)}, bf16[22,3,768]{2,1,0:T(4,128)(2,1)S(1)}, u32[]{:S(2)}, u32[]{:S(2)}) %collective-permute-start.3) | collective-permute-done | bytes 101408 | tf_op jit(solution)/shard_map/ppermute | solution.py:27
  33.2 0.4 maximum_convert_fusion
  33.6 12.3 %fusion.111 = (f32[16,24]{1,0:T(8,128)S(1)}, f32[16,24,768]{2,1,0:T(8,128)S(1)}) fusion(f32[768]{0:T(1024)S(1)} %get-tuple-element.49, f32[22,30,768]{2,1,0:T(8,128)S(1)} %maximum_convert_fusion, f32[768]{0:T(1024)S(1)} %get-tuple-element.50, f32[768]{0:T(1024)S(1)} %get-tuple-element.3, f32[768]{0:T(1024)S(1)} %get-tuple-element.4, ...), kind=kLoop, calls=%fused_computation.227 | loop fusion | flops 28900992 | bytes 59134464 | tf_op jit(solution)/shard_map/reduce_sum | solution.py:47
  45.9 0.3 multiply_reduce_fusion
  46.2 0.4 copy-done.8
  46.8 57.7 %all-gather.4.cloned.1.call-done = bf16[768,3072]{1,0:T(8,128)(2,1)} async-done(((bf16[768,768]{1,0:T(8,128)(2,1)}), bf16[768,3072]{1,0:T(8,128)(2,1)}) %all-gather.4.cloned.1.call-update) | async-done | bytes 4718608 | tf_op jit(solution)/shard_map/all_gather | solution.py:69
  104.6 89.4 %all-gather.6.cloned.1.call-done = bf16[3072,768]{1,0:T(8,128)(2,1)} async-done(((bf16[768,768]{1,0:T(8,128)(2,1)}), bf16[3072,768]{1,0:T(8,128)(2,1)}) %all-gather.6.cloned.1.call-update) | async-done | bytes 4718608 | tf_op jit(solution)/shard_map/all_gather | solution.py:74
  193.9 7.9 %fusion.34 = bf16[384,768]{1,0:T(8,128)(2,1)S(1)} fusion(bf16[3072,768]{1,0:T(8,128)(2,1)} %all-gather.6.cloned.1.call-done, bf16[384,768]{1,0:T(8,128)(2,1)S(1)} %bitcast.76, bf16[384,768]{1,0:T(8,128)(2,1)S(1)} %bitcast.80, bf16[768,3072]{1,0:T(8,128)(2,1)} %all-gather.4.cloned.1.call-done), kind=kOutput, calls=%fused_computation.38 | convolution fusion | flops 3635380224 | bytes 11206656 | tf_op jit(solution)/shard_map/dot_general | solution.py:73
  201.9 42.4 %all-gather.8.cloned.1.call-done = bf16[768,1536]{1,0:T(8,128)(2,1)} async-done(((bf16[768,384]{1,0:T(8,128)(2,1)}), bf16[768,1536]{1,0:T(8,128)(2,1)}) %all-gather.8.cloned.1.call-update) | async-done | bytes 2359312 | tf_op jit(solution)/shard_map/all_gather | solution.py:80
  244.2 2.7 convolution_convert_fusion
  247.0 0.9 fusion.113
  247.9 1.0 copy.23
  248.9 1.8 bitcast_reduce_fusion
  250.8 2.3 bitcast_reduce_fusion.1
  253.0 2.3 bitcast_reduce_fusion.2
  255.4 2.1 copy.22
  257.5 3.6 fusion.37
  261.1 3.0 fusion.11
  264.1 1.5 fusion.40
  265.6 0.5 fusion.15
  266.2 1.5 fusion.43
  267.6 39.0 %pmax.7 = f32[512,12]{0,1:T(8,128)S(1)} all-reduce(f32[512,12]{0,1:T(8,128)S(1)} %pad_maximum_fusion.1), channel_id=1, replica_groups=mesh['row'=8,'col'=4] {'row','col'}, use_global_device_ids=true, to_apply=%region_5.6 | all-reduce | flops 6144 | bytes 49152 | tf_op jit(solution)/shard_map/pmax | solution.py:122
  306.6 0.6 maximum_multiply_fusion.1
  307.3 2.7 maximum_multiply_fusion
  310.0 0.9 copy-done.6
  310.9 1.7 collective-permute-start.4
  312.6 10.9 %collective-permute-done.4 = bf16[768,192]{0,1:T(8,128)(2,1)S(1)} collective-permute-done((bf16[768,192]{0,1:T(8,128)(2,1)S(1)}, bf16[768,192]{0,1:T(8,128)(2,1)S(1)}, u32[]{:S(2)}, u32[]{:S(2)}) %collective-permute-start.4) | collective-permute-done | bytes 294944 | tf_op jit(solution)/shard_map/ppermute | solution.py:87
  323.5 2.5 collective-permute-start.5
  325.9 13.8 %collective-permute-done.5 = bf16[768,192]{0,1:T(8,128)(2,1)S(1)} collective-permute-done((bf16[768,192]{0,1:T(8,128)(2,1)S(1)}, bf16[768,192]{0,1:T(8,128)(2,1)S(1)}, u32[]{:S(2)}, u32[]{:S(2)}) %collective-permute-start.5) | collective-permute-done | bytes 294944 | tf_op jit(solution)/shard_map/ppermute | solution.py:87
  339.7 4.0 collective-permute-start.6
  343.8 16.0 %reduce-scatter.3.cloned.1.call-done = f32[128,768]{0,1:T(8,128)} async-done(((f32[512,768]{0,1:T(8,128)}), f32[128,768]{0,1:T(8,128)}) %reduce-scatter.3.cloned.1.call-update) | async-done | bytes 393232 | tf_op jit(solution)/shard_map/reduce_scatter | solution.py:128
  359.9 0.6 gather_fusion
  360.6 19.6 %reduce-scatter.5.cloned.1.call-done = f32[128,12]{0,1:T(8,128)} async-done(((f32[512,12]{0,1:T(8,128)}), f32[128,12]{0,1:T(8,128)}) %reduce-scatter.5.cloned.1.call-update) | async-done | bytes 6160 | tf_op jit(solution)/shard_map/reduce_scatter | solution.py:127
  380.2 12.2 %psum.15 = f32[128,12]{0,1:T(8,128)S(1)} all-reduce(f32[128,12]{0,1:T(8,128)} %reduce-scatter.5.cloned.1.call-done), channel_id=1, replica_groups=mesh['row'=8,'col'=4] {'row'}, use_global_device_ids=true, to_apply=%region_12.13 | all-reduce | flops 1536 | bytes 12288 | tf_op jit(solution)/shard_map/psum | solution.py:130
  392.4 43.3 %all-reduce.2.cloned.1.call-done = f32[128,768]{0,1:T(8,128)} async-done(((f32[128,768]{0,1:T(8,128)}), f32[128,768]{0,1:T(8,128)}) %all-reduce.2.cloned.1.call-update) | async-done | bytes 393232 | tf_op jit(solution)/shard_map/psum | solution.py:130
  435.7 1.1 multiply_reduce_fusion.1
  436.8 0.6 convolution_convert_fusion.1
  437.5 19.5 %all_gather.15 = bf16[512,768]{1,0:T(8,128)(2,1)S(1)} all-gather(bf16[128,768]{1,0:T(8,128)(2,1)S(1)} %convolution_convert_fusion.1), channel_id=1, replica_groups=mesh['row'=8,'col'=4] {'col'}, dimensions={0}, use_global_device_ids=true | all-gather | bytes 983040 | tf_op jit(solution)/shard_map/all_gather | solution.py:134
  457.0 0.9 copy.35
  (50 shorter events, 1.4 us)
Async XLA Ops:
  7.2 1.6 copy-start.1
  7.2 97.4 %all-gather.4.cloned.1.call-start = ((), (), s32[]{:S(2)}) async-start(), calls=%async_computation.2 | async-start | bytes 5898240 | tf_op jit(solution)/shard_map/all_gather | solution.py:69
  7.9 4.6 copy-start.7
  7.9 4.8 %copy-start.2 = (bf16[512,768]{1,0:T(8,128)(2,1)S(1)}, bf16[512,768]{1,0:T(8,128)(2,1)}, u32[]{:S(2)}) copy-start(bf16[512,768]{1,0:T(8,128)(2,1)} %param.17) | copy-start | bytes 2359300
  7.9 186.0 %all-gather.6.cloned.1.call-start = ((), (), s32[]{:S(2)}) async-start(), calls=%async_computation.3 | async-start | bytes 5898240 | tf_op jit(solution)/shard_map/all_gather | solution.py:74
  8.7 235.6 %all-gather.8.cloned.1.call-start = ((), (), s32[]{:S(2)}) async-start(), calls=%async_computation.4 | async-start | bytes 2949120 | tf_op jit(solution)/shard_map/all_gather | solution.py:80
  8.8 5.3 %collective-permute-start = (bf16[3,24,768]{2,1,0:T(8,128)(2,1)S(1)}, bf16[3,24,768]{2,1,0:T(8,128)(2,1)S(1)}, u32[]{:S(2)}, u32[]{:S(2)}) collective-permute-start(bf16[3,24,768]{2,1,0:T(8,128)(2,1)S(1)} %get-tuple-element.62), channel_id=1, source_target_pairs={{0,4},{4,8},{8,12},{12,16},{16,20},{20,24},{24,28},{1,5},{5,9},{9,... | collective-permute-start | bytes 331784 | tf_op jit(solution)/shard_map/ppermute | solution.py:25
  11.2 5.3 %collective-permute-start.1 = (bf16[3,24,768]{2,1,0:T(8,128)(2,1)S(1)}, bf16[3,24,768]{2,1,0:T(8,128)(2,1)S(1)}, u32[]{:S(2)}, u32[]{:S(2)}) collective-permute-start(bf16[3,24,768]{2,1,0:T(8,128)(2,1)S(1)} %get-tuple-element.61), channel_id=1, source_target_pairs={{4,0},{8,4},{12,8},{16,12},{20,16},{24,20},{28,24},{5,1},{9,5},{13... | collective-permute-start | bytes 331784 | tf_op jit(solution)/shard_map/ppermute | solution.py:27
  12.5 347.2 %reduce-scatter.3.cloned.1.call-start = ((), (), s32[]{:S(2)}) async-start(), calls=%async_computation.5 | async-start | bytes 1966080 | tf_op jit(solution)/shard_map/reduce_scatter | solution.py:128
  16.6 9.2 %collective-permute-start.2 = (bf16[22,3,768]{2,1,0:T(4,128)(2,1)S(1)}, bf16[22,3,768]{2,1,0:T(4,128)(2,1)S(1)}, u32[]{:S(2)}, u32[]{:S(2)}) collective-permute-start(bf16[22,3,768]{2,1,0:T(4,128)(2,1)S(1)} %get-tuple-element.59), channel_id=1, source_target_pairs={{0,1},{1,2},{2,3},{4,5},{5,6},{6,7},{8,9},{9,10},{10,11},{12,13},{... | collective-permute-start | bytes 304136 | tf_op jit(solution)/shard_map/ppermute | solution.py:25
  20.1 13.1 %collective-permute-start.3 = (bf16[22,3,768]{2,1,0:T(4,128)(2,1)S(1)}, bf16[22,3,768]{2,1,0:T(4,128)(2,1)S(1)}, u32[]{:S(2)}, u32[]{:S(2)}) collective-permute-start(bf16[22,3,768]{2,1,0:T(4,128)(2,1)S(1)} %get-tuple-element.60), channel_id=1, source_target_pairs={{1,0},{2,1},{3,2},{5,4},{6,5},{7,6},{9,8},{10,9},{11,10},{13,12},{... | collective-permute-start | bytes 304136 | tf_op jit(solution)/shard_map/ppermute | solution.py:27
  45.9 0.7 copy-start.8
  45.9 0.7 copy-start.9
  201.9 45.1 %copy-start.11 = (bf16[384,768]{1,0:T(8,128)(2,1)}, bf16[384,768]{1,0:T(8,128)(2,1)S(1)}, u32[]{:S(2)}) copy-start(bf16[384,768]{1,0:T(8,128)(2,1)S(1)} %fusion.34) | copy-start | bytes 1769476
  248.9 1.8 copy-start.3
  248.9 1.8 copy-start.5
  257.5 3.6 copy-start
  261.1 3.0 copy-start.4
  310.0 1.0 copy-start.6
  310.0 70.2 %reduce-scatter.5.cloned.1.call-start = ((), (), s32[]{:S(2)}) async-start(), calls=%async_computation.7 | async-start | bytes 40960 | tf_op jit(solution)/shard_map/reduce_scatter | solution.py:127
  310.9 12.5 %collective-permute-start.4 = (bf16[768,192]{0,1:T(8,128)(2,1)S(1)}, bf16[768,192]{0,1:T(8,128)(2,1)S(1)}, u32[]{:S(2)}, u32[]{:S(2)}) collective-permute-start(bf16[768,192]{0,1:T(8,128)(2,1)S(1)} %copy-done.6), channel_id=1, source_target_pairs={{0,1},{1,2},{2,3},{3,0},{4,5},{5,6},{6,7},{7,4},{8,9},{9,10},{10,1... | collective-permute-start | bytes 884744 | tf_op jit(solution)/shard_map/ppermute | solution.py:87
  323.5 16.2 %collective-permute-start.5 = (bf16[768,192]{0,1:T(8,128)(2,1)S(1)}, bf16[768,192]{0,1:T(8,128)(2,1)S(1)}, u32[]{:S(2)}, u32[]{:S(2)}) collective-permute-start(bf16[768,192]{0,1:T(8,128)(2,1)S(1)} %collective-permute-done.4), channel_id=1, source_target_pairs={{0,1},{1,2},{2,3},{3,0},{4,5},{5,6},{6,7},{7,4},{8,9},{9,10},{10,1... | collective-permute-start | bytes 884744 | tf_op jit(solution)/shard_map/ppermute | solution.py:87
  339.7 20.0 %collective-permute-start.6 = (bf16[768,192]{0,1:T(8,128)(2,1)S(1)}, bf16[768,192]{0,1:T(8,128)(2,1)S(1)}, u32[]{:S(2)}, u32[]{:S(2)}) collective-permute-start(bf16[768,192]{0,1:T(8,128)(2,1)S(1)} %collective-permute-done.5), channel_id=1, source_target_pairs={{0,1},{1,2},{2,3},{3,0},{4,5},{5,6},{6,7},{7,4},{8,9},{9,10},{10,1... | collective-permute-start | bytes 884744 | tf_op jit(solution)/shard_map/ppermute | solution.py:87
  343.7 92.0 %all-reduce.2.cloned.1.call-start = ((), (), s32[]{:S(2)}) async-start(), calls=%async_computation.6 | async-start | bytes 786432 | tf_op jit(solution)/shard_map/psum | solution.py:130
  359.9 76.9 %copy-start.10 = (f32[768]{0:T(1024)S(1)}, f32[768]{0:T(1024)}, u32[]{:S(2)}) copy-start(f32[768]{0:T(1024)} %param.18) | copy-start | bytes 9220
Sparse Core Ops, SparseCore 0:
  9.6 94.9 all-gather.3
  106.1 87.7 all-gather.5
  195.6 48.6 all-gather.7
  310.1 49.5 reduce-scatter.2
  361.8 18.3 reduce-scatter.4
  383.1 52.5 all-reduce.1
